TPU v7x, 32 devices: a whole 2x2x4 slice. The times are simulated.
32 devices in a mesh: groups: 2 (over y), blk: 4 (over z), head: 2 (over x), pair: 2 (over core).
Axes of the slice: x: 2, y: 2, z: 4, core: 2. Of those that a mesh axis runs over, the one named last changes fastest.
Arguments:
- single: bfloat16 [256, 384], P(('groups', 'blk')), parts along dimension 0, may hold values from -6 to 6
- pair: bfloat16 [256, 4, 32, 128], P(('groups', 'blk'), None, 'pair'), parts along dimension 0, may hold values from -6 to 6
- frames: float32 [12, 256], P(None, ('groups', 'blk')), parts along dimension 1, as said below
- chain: int32 [256], P(('groups', 'blk')), parts along dimension 0, may hold values from 0 to 5, never falling along the last dimension, each value on 1 to 42 neighbouring positions
- mask: int32 [256], P(('groups', 'blk')), parts along dimension 0, may hold values 0 or 1
- w_query: bfloat16 [384, 192], P(None, 'head'), may hold values from -0.3125 to 0.3125
- w_key_value: bfloat16 [384, 384], P(None, 'head'), may hold values from -0.3125 to 0.3125
- w_query_points: bfloat16 [384, 144], P(None, 'head'), may hold values from -0.3125 to 0.3125
- w_kv_points: bfloat16 [384, 432], P(None, 'head'), may hold values from -0.3125 to 0.3125
- w_pair_bias: bfloat16 [128, 12], P(None, 'head'), may hold values from -0.5 to 0.5
- head_weights: float32 [12], P('head'), may hold values from -9 to 1
- chain_bias: float32 [12], P('head'), may hold values from -3 to 3
- w_out: bfloat16 [12, 176, 384], P('head'), may hold values from -0.125 to 0.125
- out_gain: float32 [384], replicated, may hold values from 0.5 to 1.5
- w_backbone: bfloat16 [384, 6], replicated, may hold values from -0.3125 to 0.3125
Outputs:
- single_out: bfloat16 [256, 384], P(('groups', 'blk')), parts along dimension 0
- frames_out: float32 [12, 256], P(None, 'groups'), parts along dimension 1
There are 2 independent parts, one for each index of `groups`. A program takes and returns all parts, laid end to end along the dimension named above; an argument that names none is the same for every part. Nothing has to cross between parts.
Inputs may be any that keep to these rules, and one draw needn't show every extreme that they name: `frames`: rows 0 to 8 of every column hold an orthonormal rotation matrix row by row; rows 9 to 11 the translation.
All inputs are finite; a program needn't handle non-finite values. No bound on the sum of `mask` on one device may be relied on, other than what follows from the above.
Results may differ from a plain program's by a relative error of at most 0.0048.
Values sent between devices are 32-bit elements; how exact they have to be, the bound alone decides.
A program may use at most 64 MiB of HBM per device.

v0:
```python
import math
import jax
import jax.numpy as jnp
from jax import lax
from jax.sharding import PartitionSpec as P

HIGH = lax.Precision.HIGHEST
LOGIT_WEIGHT = math.sqrt(1.0 / 3.0)
MASK_PENALTY = 100000.0


def shifted(array, axis, by):
    peers = lax.axis_size(axis)
    return lax.ppermute(array, axis, [(i, (i + by) % peers) for i in range(peers)])


def combined_all(value, axis, join):
    pieces = jax.tree.map(lambda part: lax.all_gather(part, axis), value)
    head = jax.tree.map(lambda part: part[0], pieces)
    tail = jax.tree.map(lambda part: part[1:], pieces)
    so_far, _ = lax.scan(lambda so_far, section: (join(so_far, section), None), head, tail)
    return so_far


def to_global(local, frames):
    rotation = frames[:9].reshape(3, 3, -1)
    moved = jnp.einsum("abn,ngb->nga", rotation, local, precision=HIGH)
    return moved + jnp.transpose(frames[9:12])[:, None, :]


def to_local(points, frames):
    rotation = frames[:9].reshape(3, 3, -1)
    moved = points - jnp.transpose(frames[9:12])[:, None, None, :]
    return jnp.einsum("abn,nhpa->nhpb", rotation, moved, precision=HIGH)


def compose(frames, motion):
    rotation = frames[:9].reshape(3, 3, -1)
    inverse = 1.0 / jnp.sqrt(1.0 + motion[:, 0] ** 2 + motion[:, 1] ** 2 + motion[:, 2] ** 2)
    quat_b = motion[:, 0] * inverse
    quat_c = motion[:, 1] * inverse
    quat_d = motion[:, 2] * inverse
    spin = jnp.stack(
        [
            inverse * inverse + quat_b * quat_b - quat_c * quat_c - quat_d * quat_d,
            2.0 * (quat_b * quat_c - inverse * quat_d),
            2.0 * (quat_b * quat_d + inverse * quat_c),
            2.0 * (quat_b * quat_c + inverse * quat_d),
            inverse * inverse - quat_b * quat_b + quat_c * quat_c - quat_d * quat_d,
            2.0 * (quat_c * quat_d - inverse * quat_b),
            2.0 * (quat_b * quat_d - inverse * quat_c),
            2.0 * (quat_c * quat_d + inverse * quat_b),
            inverse * inverse - quat_b * quat_b - quat_c * quat_c + quat_d * quat_d,
        ]
    ).reshape(3, 3, -1)
    new_rotation = jnp.einsum("abn,bcn->acn", rotation, spin, precision=HIGH)
    offset = jnp.einsum("abn,nb->an", rotation, motion[:, 3:6], precision=HIGH)
    return jnp.concatenate([new_rotation.reshape(9, -1), frames[9:12] + offset], axis=0)


def attention_logits(
    pair_rows,
    query_rows,
    query_points,
    query_chain,
    query_present,
    keys,
    key_points,
    key_chain,
    key_present,
    w_pair_bias,
    distance_scale,
    chain_bias,
):
    count_q = pair_rows.shape[0]
    count_k = pair_rows.shape[1]
    bias = jnp.dot(
        pair_rows.reshape(count_q * count_k, -1), w_pair_bias, preferred_element_type=jnp.float32
    ).reshape(count_q, count_k, -1)
    dots = jnp.einsum("ihc,jhc->ijh", query_rows, keys, precision=HIGH) / math.sqrt(keys.shape[-1])
    gaps = query_points[:, None] - key_points[None]
    distance = jnp.sum(gaps * gaps, axis=(3, 4))
    differ = (query_chain[:, None] != key_chain[None, :]).astype(jnp.float32)
    logits = LOGIT_WEIGHT * (
        dots + bias - distance_scale * distance + chain_bias * differ[..., None]
    )
    absent = 1.0 - query_present[:, None] * key_present[None, :]
    return logits - MASK_PENALTY * absent[..., None]


def rescale(values, factor):
    return values * factor.reshape(factor.shape + (1,) * (values.ndim - factor.ndim))


def fold_pair(first, second):
    best = jnp.maximum(first[0], second[0])
    first_scale = jnp.exp(first[0] - best)
    second_scale = jnp.exp(second[0] - best)
    merged = [
        rescale(left_part, first_scale) + rescale(right_part, second_scale)
        for left_part, right_part in zip(first[1:], second[1:])
    ]
    return (best,) + tuple(merged)


def body(
    single,
    pair,
    frames,
    chain,
    mask,
    w_query,
    w_key_value,
    w_query_points,
    w_kv_points,
    w_pair_bias,
    head_weights,
    chain_bias,
    w_out,
    out_gain,
    w_backbone,
):
    rows = single.shape[0]
    half = pair.shape[2]
    width = pair.shape[3]
    heads_here = w_pair_bias.shape[1]
    head_size = w_query.shape[1] // heads_here
    query_count = w_query_points.shape[1] // (3 * heads_here)
    value_count = w_kv_points.shape[1] // (3 * heads_here) - query_count
    pair_keys = pair.reshape(rows, pair.shape[1] * half, width)
    query = jnp.dot(single, w_query, preferred_element_type=jnp.float32).reshape(
        rows, heads_here, head_size
    )
    query_local = jnp.dot(single, w_query_points, preferred_element_type=jnp.float32)
    query_points = to_global(query_local.reshape(rows, heads_here * query_count, 3), frames)
    query_points = query_points.reshape(rows, heads_here, query_count, 3)
    query_chain = chain.astype(jnp.float32)
    query_present = mask.astype(jnp.float32)
    distance_scale = jax.nn.softplus(head_weights) * math.sqrt(2.0 / (9.0 * query_count)) / 2.0
    position = lax.axis_index("pair")
    key_single = lax.dynamic_slice_in_dim(single, position * half, half, 0)
    key_frames = lax.dynamic_slice_in_dim(frames, position * half, half, 1)
    key_chain = lax.dynamic_slice_in_dim(query_chain, position * half, half, 0)
    key_present = lax.dynamic_slice_in_dim(query_present, position * half, half, 0)
    key_value = jnp.dot(key_single, w_key_value, preferred_element_type=jnp.float32)
    key_local = jnp.dot(key_single, w_kv_points, preferred_element_type=jnp.float32)
    key_global = to_global(
        key_local.reshape(half, heads_here * (query_count + value_count), 3), key_frames
    )
    payload = jnp.concatenate([key_value, key_global.reshape(half, -1)], axis=1)
    key_meta = jnp.stack([key_chain, key_present], axis=1)
    split_at = heads_here * 2 * head_size

    def absorb(carry, moving, moving_meta, start):
        top, total, sum_values, sum_points, sum_pair = carry
        count = moving.shape[0]
        pieces = moving[:, :split_at].reshape(count, heads_here, 2, head_size)
        points = moving[:, split_at:].reshape(count, heads_here, query_count + value_count, 3)
        pair_rows = lax.dynamic_slice_in_dim(pair_keys, start, count, 1)
        logits = attention_logits(
            pair_rows,
            query,
            query_points,
            query_chain,
            query_present,
            pieces[:, :, 0],
            points[:, :, :query_count],
            moving_meta[:, 0],
            moving_meta[:, 1],
            w_pair_bias,
            distance_scale,
            chain_bias,
        )
        new_top = jnp.maximum(top, jnp.max(logits, axis=1))
        scale = jnp.exp(top - new_top)
        weights = jnp.exp(logits - new_top[:, None, :])
        total = total * scale + jnp.sum(weights, axis=1)
        sum_values = sum_values * scale[..., None] + jnp.einsum(
            "ijh,jhc->ihc", weights, pieces[:, :, 1], precision=HIGH
        )
        sum_points = sum_points * scale[..., None, None] + jnp.einsum(
            "ijh,jhpd->ihpd", weights, points[:, :, query_count:], precision=HIGH
        )
        sum_pair = sum_pair * scale[..., None] + jnp.einsum(
            "ijh,ijc->ihc",
            weights.astype(jnp.bfloat16),
            pair_rows,
            preferred_element_type=jnp.float32,
        )
        return (new_top, total, sum_values, sum_points, sum_pair)

    initial = (
        jnp.full((rows, heads_here), -1e30, jnp.float32),
        jnp.zeros((rows, heads_here), jnp.float32),
        jnp.zeros((rows, heads_here, head_size), jnp.float32),
        jnp.zeros((rows, heads_here, value_count, 3), jnp.float32),
        jnp.zeros((rows, heads_here, width), jnp.float32),
    )
    block = lax.axis_index("blk")
    blocks = lax.axis_size("blk")
    carry = absorb(initial, payload, key_meta, block * half)

    def advance(step, state):
        carry, moving, moving_meta = state
        moving, moving_meta = shifted((moving, moving_meta), "blk", 1)
        source = (block - step) % blocks
        return (absorb(carry, moving, moving_meta, source * half), moving, moving_meta)

    carry = lax.fori_loop(1, blocks, advance, (carry, payload, key_meta))[0]
    best, total, sum_values, sum_points, sum_pair = combined_all(carry, "pair", fold_pair)
    attended = sum_values / total[..., None]
    pointed = to_local(sum_points / total[..., None, None], frames)
    point_norms = jnp.sqrt(jnp.sum(pointed * pointed, axis=3) + 1.0)
    paired = sum_pair / total[..., None]
    joined = jnp.concatenate(
        [attended, pointed.reshape(rows, heads_here, value_count * 3), point_norms, paired], axis=2
    ).astype(jnp.bfloat16)
    partial_update = jnp.dot(
        joined.reshape(rows, -1),
        w_out.reshape(-1, w_out.shape[2]),
        preferred_element_type=jnp.float32,
    )
    update = lax.psum(partial_update, "head")
    mixed = single.astype(jnp.float32) + update
    centre = jnp.mean(mixed, axis=1, keepdims=True)
    spread = jnp.mean(jnp.square(mixed - centre), axis=1, keepdims=True)
    single_out = ((mixed - centre) * lax.rsqrt(spread + 1e-05) * out_gain).astype(jnp.bfloat16)
    motion = jnp.dot(single_out, w_backbone, preferred_element_type=jnp.float32)
    frames_new = compose(frames, motion)
    frames_out = lax.all_gather(frames_new, "blk", axis=1, tiled=True)
    return (single_out, frames_out)


def solution(mesh):
    placed = (
        P(("groups", "blk"), None),
        P(("groups", "blk"), None, "pair", None),
        P(None, ("groups", "blk")),
        P(("groups", "blk")),
        P(("groups", "blk")),
        P(None, "head"),
        P(None, "head"),
        P(None, "head"),
        P(None, "head"),
        P(None, "head"),
        P("head"),
        P("head"),
        P("head", None, None),
        P(),
        P(),
    )
    return jax.shard_map(
        body,
        mesh=mesh,
        in_specs=placed,
        out_specs=(P(("groups", "blk"), None), P(None, "groups")),
        check_vma=False,
    )
```

profile of v0, /device:TPU:0, one launch (start us, length us, event | category | flops | bytes accessed | tf_op | source)
XLA Modules:
  0.0 85.5 jit_solution(7720689807309747148)
XLA Ops:
  0.7 0.7 copy-done.13
  1.7 0.3 copy-done.8
  2.6 0.6 copy-done.3
  3.1 1.1 %fusion.59 = f32[16,192]{1,0:T(8,128)S(1)} fusion(bf16[384,192]{0,1:T(8,128)(2,1)} %param.23, bf16[32,384]{1,0:T(8,128)(2,1)S(1)} %copy-done.3, s32[]{:T(128)S(6)} %select_n.43), kind=kOutput, calls=%fused_computation.96 | convolution fusion | flops 2359296 | bytes 172036 | tf_op jit(solution)/shard_map/dot_general | solution.py:145
  4.6 0.8 copy-done.7
  5.7 0.3 convolution_add_fusion.2
  6.6 0.7 copy-done.4
  8.4 0.3 copy-done.2
  8.7 0.3 copy-done.6
  9.0 0.4 fusion.35
  10.1 0.4 copy-done.10
  11.6 0.4 fusion.20
  12.0 35.5 %while.7 = (s32[]{:T(128)}, f32[32,6]{0,1:T(8,128)S(1)}, f32[32,6]{0,1:T(8,128)S(1)}, f32[32,6,16]{0,2,1:T(8,128)S(1)}, f32[32,6,8,3]{0,2,3,1:T(8,128)S(1)}, /*i...) while((s32[]{:T(128)}, f32[32,6]{0,1:T(8,128)S(1)}, ...), condition=%wide.region_7.8_spmd, body=%wide.region_3.7_spmd.sunk | while | flops 3855250 | bytes 1648512 | solution.py:209
  12.0 3.1 %collective-permute-start = (f32[16,2]{0,1:T(2,128)S(1)}, f32[16,2]{0,1:T(2,128)S(1)}, u32[]{:S(2)}, u32[]{:S(2)}) collective-permute-start(f32[16,2]{0,1:T(2,128)S(1)} %get-tuple-element.757), channel_id=1, source_target_pairs={{0,4},{4,8},{8,12},{12,0},{1,5},{5,9},{9,13},{13,1},{2,6},{6,10},{... | collective-permute-start | bytes 392 | tf_op jit(solution)/shard_map/while/body/eval_jaxpr/ppermute | solution.py:14
  15.1 1.6 %collective-permute-start.1 = (f32[16,408]{0,1:T(8,128)S(1)}, f32[16,408]{0,1:T(8,128)S(1)}, u32[]{:S(2)}, u32[]{:S(2)}) collective-permute-start(f32[16,408]{0,1:T(8,128)S(1)} %get-tuple-element.756), channel_id=1, source_target_pairs={{0,4},{4,8},{8,12},{12,0},{1,5},{5,9},{9,13},{13,1},{2,6},{6,10},{... | collective-permute-start | bytes 78344 | tf_op jit(solution)/shard_map/while/body/eval_jaxpr/ppermute | solution.py:14
  16.7 0.4 fusion.127
  17.2 1.5 %collective-permute-done = f32[16,2]{0,1:T(2,128)S(1)} collective-permute-done((f32[16,2]{0,1:T(2,128)S(1)}, f32[16,2]{0,1:T(2,128)S(1)}, u32[]{:S(2)}, u32[]{:S(2)}) %collective-permute-start) | collective-permute-done | bytes 160 | tf_op jit(solution)/shard_map/while/body/eval_jaxpr/ppermute | solution.py:14
  18.9 4.7 %collective-permute-done.1 = f32[16,408]{0,1:T(8,128)S(1)} collective-permute-done((f32[16,408]{0,1:T(8,128)S(1)}, f32[16,408]{0,1:T(8,128)S(1)}, u32[]{:S(2)}, u32[]{:S(2)}) %collective-permute-start.1) | collective-permute-done | bytes 26144 | tf_op jit(solution)/shard_map/while/body/eval_jaxpr/ppermute | solution.py:14
  23.7 0.6 copy-done.1
  24.5 0.3 fusion.128
  25.3 0.6 slice-done
  26.5 1.4 %collective-permute-start.1 = (f32[16,408]{0,1:T(8,128)S(1)}, f32[16,408]{0,1:T(8,128)S(1)}, u32[]{:S(2)}, u32[]{:S(2)}) collective-permute-start(f32[16,408]{0,1:T(8,128)S(1)} %get-tuple-element.756), channel_id=1, source_target_pairs={{0,4},{4,8},{8,12},{12,0},{1,5},{5,9},{9,13},{13,1},{2,6},{6,10},{... | collective-permute-start | bytes 78344 | tf_op jit(solution)/shard_map/while/body/eval_jaxpr/ppermute | solution.py:14
  27.8 0.4 fusion.127
  28.3 3.5 %collective-permute-done = f32[16,2]{0,1:T(2,128)S(1)} collective-permute-done((f32[16,2]{0,1:T(2,128)S(1)}, f32[16,2]{0,1:T(2,128)S(1)}, u32[]{:S(2)}, u32[]{:S(2)}) %collective-permute-start) | collective-permute-done | bytes 160 | tf_op jit(solution)/shard_map/while/body/eval_jaxpr/ppermute | solution.py:14
  32.0 2.1 %collective-permute-done.1 = f32[16,408]{0,1:T(8,128)S(1)} collective-permute-done((f32[16,408]{0,1:T(8,128)S(1)}, f32[16,408]{0,1:T(8,128)S(1)}, u32[]{:S(2)}, u32[]{:S(2)}) %collective-permute-start.1) | collective-permute-done | bytes 26144 | tf_op jit(solution)/shard_map/while/body/eval_jaxpr/ppermute | solution.py:14
  34.2 0.6 copy-done.1
  35.9 0.6 slice-done
  36.4 0.3 fusion.131
  37.1 0.6 collective-permute-start.1
  37.7 0.4 fusion.127
  38.2 4.3 %collective-permute-done = f32[16,2]{0,1:T(2,128)S(1)} collective-permute-done((f32[16,2]{0,1:T(2,128)S(1)}, f32[16,2]{0,1:T(2,128)S(1)}, u32[]{:S(2)}, u32[]{:S(2)}) %collective-permute-start) | collective-permute-done | bytes 160 | tf_op jit(solution)/shard_map/while/body/eval_jaxpr/ppermute | solution.py:14
  42.6 2.1 %collective-permute-done.1 = f32[16,408]{0,1:T(8,128)S(1)} collective-permute-done((f32[16,408]{0,1:T(8,128)S(1)}, f32[16,408]{0,1:T(8,128)S(1)}, u32[]{:S(2)}, u32[]{:S(2)}) %collective-permute-start.1) | collective-permute-done | bytes 26144 | tf_op jit(solution)/shard_map/while/body/eval_jaxpr/ppermute | solution.py:14
  44.8 0.6 copy-done.1
  46.4 0.6 slice-done
  47.0 0.3 fusion.131
  47.6 1.8 %all-gather.5 = f32[2,32,6]{1,2,0:T(8,128)S(1)} all-gather(f32[1,32,6]{1,2,0:T(8,128)S(1)} %bitcast.281), channel_id=3, replica_groups=mesh['groups'=2,'blk'=4,'head'=2,'pair'=2] {'pair'}, dimensions={0}, use_global_device_ids=true | all-gather | bytes 2304 | tf_op jit(solution)/shard_map/all_gather | solution.py:18
  49.4 1.8 %all-gather.6 = f32[2,32,6]{1,2,0:T(8,128)S(1)} all-gather(f32[1,32,6]{1,2,0:T(8,128)S(1)} %bitcast.282), channel_id=4, replica_groups=mesh['groups'=2,'blk'=4,'head'=2,'pair'=2] {'pair'}, dimensions={0}, use_global_device_ids=true | all-gather | bytes 2304 | tf_op jit(solution)/shard_map/all_gather | solution.py:18
  51.5 1.9 %all-gather.4 = f32[64,6,128]{2,0,1:T(8,128)S(1)} all-gather(f32[32,6,128]{2,0,1:T(8,128)S(1)} %copy.259), channel_id=6, replica_groups=mesh['groups'=2,'blk'=4,'head'=2,'pair'=2] {'pair'}, dimensions={0}, use_global_device_ids=true | all-gather | bytes 294912 | tf_op jit(solution)/shard_map/all_gather | solution.py:18
  53.7 1.9 %all-gather = f32[64,6,16]{2,0,1:T(8,128)S(1)} all-gather(f32[32,6,16]{2,0,1:T(8,128)S(1)} %copy.249), channel_id=2, replica_groups=mesh['groups'=2,'blk'=4,'head'=2,'pair'=2] {'pair'}, dimensions={0}, use_global_device_ids=true | all-gather | bytes 36864 | tf_op jit(solution)/shard_map/all_gather | solution.py:18
  56.0 2.4 %all-gather.3 = f32[64,6,8,3]{2,1,3,0:T(8,128)S(1)} all-gather(f32[32,6,8,3]{2,1,3,0:T(8,128)S(1)} %copy.250), channel_id=5, replica_groups=mesh['groups'=2,'blk'=4,'head'=2,'pair'=2] {'pair'}, dimensions={0}, use_global_device_ids=true | all-gather | bytes 55296 | tf_op jit(solution)/shard_map/all_gather | solution.py:18
  58.6 1.1 %fusion.82 = (bf16[32,6,8,3]{2,3,1,0:T(4,128)(2,1)S(1)}, f32[32,6,8]{2,1,0:T(8,128)S(1)}) fusion(f32[3,3,32,1]{0,1,3,2:T(4,128)S(1)} %copy.271, f32[32,6,8,3]{2,1,3,0:T(8,128)S(1)} %fusion.30), kind=kOutput, calls=%fused_computation.152 | convolution fusion | flops 178176 | bytes 34944 | tf_op jit(solution)/shard_map/abn,nhpa->nhpb/dot_general | solution.py:34
  60.3 0.4 convolution_bitcast_fusion.4
  60.7 8.6 %psum.7 = f32[32,384]{1,0:T(8,128)S(1)} all-reduce(f32[32,384]{1,0:T(8,128)S(1)} %convolution_bitcast_fusion.4), channel_id=1, replica_groups=mesh['groups'=2,'blk'=4,'head'=2,'pair'=2] {'head'}, use_global_device_ids=true, to_apply=%region_9.10 | all-reduce | flops 12288 | bytes 98304 | tf_op jit(solution)/shard_map/psum | solution.py:223
  69.7 0.6 copy-done.11
  70.5 0.4 copy-done.5
  71.1 0.3 convolution_bitcast_fusion.3
  71.6 13.1 %all-gather.7 = f32[4,32,12]{1,2,0:T(8,128)S(1)} all-gather(f32[1,32,12]{1,2,0:T(8,128)S(1)} %maximum_bitcast_fusion), channel_id=1, replica_groups=mesh['groups'=2,'blk'=4,'head'=2,'pair'=2] {'blk'}, dimensions={0}, use_global_device_ids=true | all-gather | bytes 7680 | tf_op jit(solution)/shard_map/all_gather | solution.py:230
  84.8 0.7 reshape.714
  (176 shorter events, 11.9 us)
Async XLA Ops:
  0.6 59.6 %copy-start = (bf16[6,176,384]{2,1,0:T(8,128)(2,1)S(1)}, bf16[6,176,384]{2,1,0:T(8,128)(2,1)}, u32[]{:S(2)}) copy-start(bf16[6,176,384]{2,1,0:T(8,128)(2,1)} %param.29) | copy-start | bytes 2433028
  0.7 0.7 copy-start.13
  0.7 0.7 copy-start.14
  0.7 0.7 copy-start.15
  1.4 0.7 copy-start.8
  2.4 0.7 copy-start.3
  3.1 1.2 %copy-start.9 = (bf16[384,72]{0,1:T(8,128)(2,1)S(1)}, bf16[384,72]{0,1:T(8,128)(2,1)}, u32[]{:S(2)}) copy-start(bf16[384,72]{0,1:T(8,128)(2,1)} %param.24) | copy-start | bytes 165892
  4.5 0.9 %copy-start.7 = (bf16[384,96]{0,1:T(8,128)(2,1)S(1)}, bf16[384,96]{0,1:T(8,128)(2,1)}, u32[]{:S(2)}) copy-start(bf16[384,96]{0,1:T(8,128)(2,1)} %param.22) | copy-start | bytes 221188
  6.5 0.9 %copy-start.4 = (bf16[384,216]{0,1:T(8,128)(2,1)S(1)}, bf16[384,216]{0,1:T(8,128)(2,1)}, u32[]{:S(2)}) copy-start(bf16[384,216]{0,1:T(8,128)(2,1)} %param.25) | copy-start | bytes 497668
  7.6 1.0 %copy-start.2 = (bf16[32,4,16,128]{3,2,1,0:T(8,128)(2,1)S(1)}, bf16[32,4,16,128]{3,2,1,0:T(8,128)(2,1)}, u32[]{:S(2)}) copy-start(bf16[32,4,16,128]{3,2,1,0:T(8,128)(2,1)} %param.18) | copy-start | bytes 1572868
  8.3 0.7 copy-start.6
  9.8 0.7 copy-start.10
  12.0 6.7 %collective-permute-start = (f32[16,2]{0,1:T(2,128)S(1)}, f32[16,2]{0,1:T(2,128)S(1)}, u32[]{:S(2)}, u32[]{:S(2)}) collective-permute-start(f32[16,2]{0,1:T(2,128)S(1)} %get-tuple-element.757), channel_id=1, source_target_pairs={{0,4},{4,8},{8,12},{12,0},{1,5},{5,9},{9,13},{13,1},{2,6},{6,10},{... | collective-permute-start | bytes 392 | tf_op jit(solution)/shard_map/while/body/eval_jaxpr/ppermute | solution.py:14
  15.1 8.4 %collective-permute-start.1 = (f32[16,408]{0,1:T(8,128)S(1)}, f32[16,408]{0,1:T(8,128)S(1)}, u32[]{:S(2)}, u32[]{:S(2)}) collective-permute-start(f32[16,408]{0,1:T(8,128)S(1)} %get-tuple-element.756), channel_id=1, source_target_pairs={{0,4},{4,8},{8,12},{12,0},{1,5},{5,9},{9,13},{13,1},{2,6},{6,10},{... | collective-permute-start | bytes 78344 | tf_op jit(solution)/shard_map/while/body/eval_jaxpr/ppermute | solution.py:14
  23.6 0.7 copy-start.1
  25.0 0.9 %slice-start = ((f32[16,6,12,3]{0,3,2,1:T(4,128)}), f32[16,6,8,3]{0,3,2,1:T(4,128)S(1)}, s32[]{:S(2)}) async-start(f32[16,6,12,3]{0,3,2,1:T(4,128)} %copy-done.1), calls=%async_computation | async-start | bytes 196608 | tf_op jit(solution)/shard_map/while/body/eval_jaxpr/slice | solution.py:182
  26.4 5.4 %collective-permute-start = (f32[16,2]{0,1:T(2,128)S(1)}, f32[16,2]{0,1:T(2,128)S(1)}, u32[]{:S(2)}, u32[]{:S(2)}) collective-permute-start(f32[16,2]{0,1:T(2,128)S(1)} %get-tuple-element.757), channel_id=1, source_target_pairs={{0,4},{4,8},{8,12},{12,0},{1,5},{5,9},{9,13},{13,1},{2,6},{6,10},{... | collective-permute-start | bytes 392 | tf_op jit(solution)/shard_map/while/body/eval_jaxpr/ppermute | solution.py:14
  26.5 7.7 %collective-permute-start.1 = (f32[16,408]{0,1:T(8,128)S(1)}, f32[16,408]{0,1:T(8,128)S(1)}, u32[]{:S(2)}, u32[]{:S(2)}) collective-permute-start(f32[16,408]{0,1:T(8,128)S(1)} %get-tuple-element.756), channel_id=1, source_target_pairs={{0,4},{4,8},{8,12},{12,0},{1,5},{5,9},{9,13},{13,1},{2,6},{6,10},{... | collective-permute-start | bytes 78344 | tf_op jit(solution)/shard_map/while/body/eval_jaxpr/ppermute | solution.py:14
  34.2 0.7 copy-start.1
  35.6 0.9 %slice-start = ((f32[16,6,12,3]{0,3,2,1:T(4,128)}), f32[16,6,8,3]{0,3,2,1:T(4,128)S(1)}, s32[]{:S(2)}) async-start(f32[16,6,12,3]{0,3,2,1:T(4,128)} %copy-done.1), calls=%async_computation | async-start | bytes 196608 | tf_op jit(solution)/shard_map/while/body/eval_jaxpr/slice | solution.py:182
  37.0 5.4 %collective-permute-start = (f32[16,2]{0,1:T(2,128)S(1)}, f32[16,2]{0,1:T(2,128)S(1)}, u32[]{:S(2)}, u32[]{:S(2)}) collective-permute-start(f32[16,2]{0,1:T(2,128)S(1)} %get-tuple-element.757), channel_id=1, source_target_pairs={{0,4},{4,8},{8,12},{12,0},{1,5},{5,9},{9,13},{13,1},{2,6},{6,10},{... | collective-permute-start | bytes 392 | tf_op jit(solution)/shard_map/while/body/eval_jaxpr/ppermute | solution.py:14
  37.1 7.7 %collective-permute-start.1 = (f32[16,408]{0,1:T(8,128)S(1)}, f32[16,408]{0,1:T(8,128)S(1)}, u32[]{:S(2)}, u32[]{:S(2)}) collective-permute-start(f32[16,408]{0,1:T(8,128)S(1)} %get-tuple-element.756), channel_id=1, source_target_pairs={{0,4},{4,8},{8,12},{12,0},{1,5},{5,9},{9,13},{13,1},{2,6},{6,10},{... | collective-permute-start | bytes 78344 | tf_op jit(solution)/shard_map/while/body/eval_jaxpr/ppermute | solution.py:14
  44.8 0.7 copy-start.1
  46.1 0.9 %slice-start = ((f32[16,6,12,3]{0,3,2,1:T(4,128)}), f32[16,6,8,3]{0,3,2,1:T(4,128)S(1)}, s32[]{:S(2)}) async-start(f32[16,6,12,3]{0,3,2,1:T(4,128)} %copy-done.1), calls=%async_computation | async-start | bytes 196608 | tf_op jit(solution)/shard_map/while/body/eval_jaxpr/slice | solution.py:182
  60.3 9.3 %copy-start.12 = (f32[384]{0:T(512)S(1)}, f32[384]{0:T(512)}, u32[]{:S(2)}) copy-start(f32[384]{0:T(512)} %param.30) | copy-start | bytes 4612
  69.6 0.7 copy-start.11
  70.3 0.6 copy-start.5
where the time goes:
time: 86 us; the launch traced here: 85.5 us
  blocking collectives  31.6 us (37%)
  waiting for transfers between devices  18.2 us (21%)
  local copies, waits for them, and re-layouts  15 us (17%)
  matrix products  9.58 us (11%)
  starting transfers between devices  6.74 us (8%)
  other arithmetic  2.83 us (3%)
  between operations  1.1 us (1%)
    ppermute x6, waiting for transfers between devices, shifted(): lax.ppermute(array, axis, [(i, (i + by) % peers) for i in range(peers)])  18.2 us
    all_gather x1, blocking collectives, body(): frames_out = lax.all_gather(frames_new, 'blk', axis=1, tiled=True)  13.1 us
    all_gather x5, blocking collectives, combined_all(): pieces = jax.tree.map(lambda part: lax.all_gather(part, axis), value)  9.88 us
    psum x1, blocking collectives, body(): update = lax.psum(partial_update, 'head')  8.59 us
    ppermute x6, starting transfers between devices, shifted(): lax.ppermute(array, axis, [(i, (i + by) % peers) for i in range(peers)])  6.74 us
    unnamed x32, local copies, waits for them, and re-layouts  6.07 us
    while x15, local copies, waits for them, and re-layouts  1.94 us
    slice x7, local copies, waits for them, and re-layouts, absorb(): points[:, :, query_count:]  1.86 us
  transfers between devices with their start and end apart: 6, of which 6 were waited for; matrix products, arithmetic and copies ran while one was open for 2% of the time, Pallas kernels for 0%

commit v1 on v0

--- a/solution.py
+++ b/solution.py
@@ -220,7 +220,8 @@
         w_out.reshape(-1, w_out.shape[2]),
         preferred_element_type=jnp.float32,
     )
-    update = lax.psum(partial_update, "head")
+    parts = lax.all_gather(partial_update, "head", axis=0, tiled=False)
+    update = parts.sum(axis=0)
     mixed = single.astype(jnp.float32) + update
     centre = jnp.mean(mixed, axis=1, keepdims=True)
     spread = jnp.mean(jnp.square(mixed - centre), axis=1, keepdims=True)

time: 86 us -> 82.2 us (0.956)
  blocking collectives: 31.6 us -> 27.8 us
    psum x1 -> x0, blocking collectives: 8.59 us -> none  [body(): update = lax.psum(partial_update, 'head')]
    all_gather x0 -> x1, blocking collectives: none -> 4.76 us  [body(): parts = lax.all_gather(partial_update, 'head', axis=0, tiled=False)]
where the time goes in v1:
time: 82.2 us; the launch traced here: 81.6 us
  blocking collectives  27.8 us (34%)
  waiting for transfers between devices  18.2 us (22%)
  local copies, waits for them, and re-layouts  15 us (18%)
  matrix products  9.58 us (12%)
  starting transfers between devices  6.74 us (8%)
  other arithmetic  2.83 us (3%)
  between operations  1.1 us (1%)
    ppermute x6, waiting for transfers between devices, shifted(): lax.ppermute(array, axis, [(i, (i + by) % peers) for i in range(peers)])  18.2 us
    all_gather x1, blocking collectives, body(): frames_out = lax.all_gather(frames_new, 'blk', axis=1, tiled=True)  13.1 us
    all_gather x5, blocking collectives, combined_all(): pieces = jax.tree.map(lambda part: lax.all_gather(part, axis), value)  9.88 us
    ppermute x6, starting transfers between devices, shifted(): lax.ppermute(array, axis, [(i, (i + by) % peers) for i in range(peers)])  6.74 us
    unnamed x32, local copies, waits for them, and re-layouts  6.07 us
    all_gather x1, blocking collectives, body(): parts = lax.all_gather(partial_update, 'head', axis=0, tiled=False)  4.76 us
    while x15, local copies, waits for them, and re-layouts  1.94 us
    slice x7, local copies, waits for them, and re-layouts, absorb(): points[:, :, query_count:]  1.86 us
  transfers between devices with their start and end apart: 6, of which 6 were waited for; matrix products, arithmetic and copies ran while one was open for 2% of the time, Pallas kernels for 0%

profile of v1, /device:TPU:0, one launch (start us, length us, event | category | flops | bytes accessed | tf_op | source)
XLA Modules:
  0.0 81.6 jit_solution(10550850342880133612)
XLA Ops:
  0.7 0.7 copy-done.13
  1.7 0.3 copy-done.8
  2.6 0.6 copy-done.3
  3.1 1.1 %fusion.59 = f32[16,192]{1,0:T(8,128)S(1)} fusion(bf16[384,192]{0,1:T(8,128)(2,1)} %param.23, bf16[32,384]{1,0:T(8,128)(2,1)S(1)} %copy-done.3, s32[]{:T(128)S(6)} %select_n.43), kind=kOutput, calls=%fused_computation.96 | convolution fusion | flops 2359296 | bytes 172036 | tf_op jit(solution)/shard_map/dot_general | solution.py:145
  4.6 0.8 copy-done.7
  5.7 0.3 convolution_add_fusion.2
  6.6 0.7 copy-done.4
  8.4 0.3 copy-done.2
  8.7 0.3 copy-done.6
  9.0 0.4 fusion.35
  10.1 0.4 copy-done.10
  11.6 0.4 fusion.20
  12.0 35.5 %while.7 = (s32[]{:T(128)}, f32[32,6]{0,1:T(8,128)S(1)}, f32[32,6]{0,1:T(8,128)S(1)}, f32[32,6,16]{0,2,1:T(8,128)S(1)}, f32[32,6,8,3]{0,2,3,1:T(8,128)S(1)}, /*i...) while((s32[]{:T(128)}, f32[32,6]{0,1:T(8,128)S(1)}, ...), condition=%wide.region_7.8_spmd, body=%wide.region_3.7_spmd.sunk | while | flops 3855250 | bytes 1648512 | solution.py:209
  12.0 3.1 %collective-permute-start = (f32[16,2]{0,1:T(2,128)S(1)}, f32[16,2]{0,1:T(2,128)S(1)}, u32[]{:S(2)}, u32[]{:S(2)}) collective-permute-start(f32[16,2]{0,1:T(2,128)S(1)} %get-tuple-element.757), channel_id=1, source_target_pairs={{0,4},{4,8},{8,12},{12,0},{1,5},{5,9},{9,13},{13,1},{2,6},{6,10},{... | collective-permute-start | bytes 392 | tf_op jit(solution)/shard_map/while/body/eval_jaxpr/ppermute | solution.py:14
  15.1 1.6 %collective-permute-start.1 = (f32[16,408]{0,1:T(8,128)S(1)}, f32[16,408]{0,1:T(8,128)S(1)}, u32[]{:S(2)}, u32[]{:S(2)}) collective-permute-start(f32[16,408]{0,1:T(8,128)S(1)} %get-tuple-element.756), channel_id=1, source_target_pairs={{0,4},{4,8},{8,12},{12,0},{1,5},{5,9},{9,13},{13,1},{2,6},{6,10},{... | collective-permute-start | bytes 78344 | tf_op jit(solution)/shard_map/while/body/eval_jaxpr/ppermute | solution.py:14
  16.7 0.4 fusion.127
  17.2 1.5 %collective-permute-done = f32[16,2]{0,1:T(2,128)S(1)} collective-permute-done((f32[16,2]{0,1:T(2,128)S(1)}, f32[16,2]{0,1:T(2,128)S(1)}, u32[]{:S(2)}, u32[]{:S(2)}) %collective-permute-start) | collective-permute-done | bytes 160 | tf_op jit(solution)/shard_map/while/body/eval_jaxpr/ppermute | solution.py:14
  18.9 4.7 %collective-permute-done.1 = f32[16,408]{0,1:T(8,128)S(1)} collective-permute-done((f32[16,408]{0,1:T(8,128)S(1)}, f32[16,408]{0,1:T(8,128)S(1)}, u32[]{:S(2)}, u32[]{:S(2)}) %collective-permute-start.1) | collective-permute-done | bytes 26144 | tf_op jit(solution)/shard_map/while/body/eval_jaxpr/ppermute | solution.py:14
  23.7 0.6 copy-done.1
  24.5 0.3 fusion.128
  25.3 0.6 slice-done
  26.5 1.4 %collective-permute-start.1 = (f32[16,408]{0,1:T(8,128)S(1)}, f32[16,408]{0,1:T(8,128)S(1)}, u32[]{:S(2)}, u32[]{:S(2)}) collective-permute-start(f32[16,408]{0,1:T(8,128)S(1)} %get-tuple-element.756), channel_id=1, source_target_pairs={{0,4},{4,8},{8,12},{12,0},{1,5},{5,9},{9,13},{13,1},{2,6},{6,10},{... | collective-permute-start | bytes 78344 | tf_op jit(solution)/shard_map/while/body/eval_jaxpr/ppermute | solution.py:14
  27.8 0.4 fusion.127
  28.3 3.5 %collective-permute-done = f32[16,2]{0,1:T(2,128)S(1)} collective-permute-done((f32[16,2]{0,1:T(2,128)S(1)}, f32[16,2]{0,1:T(2,128)S(1)}, u32[]{:S(2)}, u32[]{:S(2)}) %collective-permute-start) | collective-permute-done | bytes 160 | tf_op jit(solution)/shard_map/while/body/eval_jaxpr/ppermute | solution.py:14
  32.0 2.1 %collective-permute-done.1 = f32[16,408]{0,1:T(8,128)S(1)} collective-permute-done((f32[16,408]{0,1:T(8,128)S(1)}, f32[16,408]{0,1:T(8,128)S(1)}, u32[]{:S(2)}, u32[]{:S(2)}) %collective-permute-start.1) | collective-permute-done | bytes 26144 | tf_op jit(solution)/shard_map/while/body/eval_jaxpr/ppermute | solution.py:14
  34.2 0.6 copy-done.1
  35.9 0.6 slice-done
  36.4 0.3 fusion.131
  37.1 0.6 collective-permute-start.1
  37.7 0.4 fusion.127
  38.2 4.3 %collective-permute-done = f32[16,2]{0,1:T(2,128)S(1)} collective-permute-done((f32[16,2]{0,1:T(2,128)S(1)}, f32[16,2]{0,1:T(2,128)S(1)}, u32[]{:S(2)}, u32[]{:S(2)}) %collective-permute-start) | collective-permute-done | bytes 160 | tf_op jit(solution)/shard_map/while/body/eval_jaxpr/ppermute | solution.py:14
  42.6 2.1 %collective-permute-done.1 = f32[16,408]{0,1:T(8,128)S(1)} collective-permute-done((f32[16,408]{0,1:T(8,128)S(1)}, f32[16,408]{0,1:T(8,128)S(1)}, u32[]{:S(2)}, u32[]{:S(2)}) %collective-permute-start.1) | collective-permute-done | bytes 26144 | tf_op jit(solution)/shard_map/while/body/eval_jaxpr/ppermute | solution.py:14
  44.8 0.6 copy-done.1
  46.4 0.6 slice-done
  47.0 0.3 fusion.131
  47.6 1.8 %all-gather.6 = f32[2,32,6]{1,2,0:T(8,128)S(1)} all-gather(f32[1,32,6]{1,2,0:T(8,128)S(1)} %bitcast.282), channel_id=3, replica_groups=mesh['groups'=2,'blk'=4,'head'=2,'pair'=2] {'pair'}, dimensions={0}, use_global_device_ids=true | all-gather | bytes 2304 | tf_op jit(solution)/shard_map/all_gather | solution.py:18
  49.4 1.8 %all-gather.7 = f32[2,32,6]{1,2,0:T(8,128)S(1)} all-gather(f32[1,32,6]{1,2,0:T(8,128)S(1)} %bitcast.284), channel_id=4, replica_groups=mesh['groups'=2,'blk'=4,'head'=2,'pair'=2] {'pair'}, dimensions={0}, use_global_device_ids=true | all-gather | bytes 2304 | tf_op jit(solution)/shard_map/all_gather | solution.py:18
  51.5 1.9 %all-gather.4 = f32[64,6,128]{2,0,1:T(8,128)S(1)} all-gather(f32[32,6,128]{2,0,1:T(8,128)S(1)} %copy.259), channel_id=6, replica_groups=mesh['groups'=2,'blk'=4,'head'=2,'pair'=2] {'pair'}, dimensions={0}, use_global_device_ids=true | all-gather | bytes 294912 | tf_op jit(solution)/shard_map/all_gather | solution.py:18
  53.7 1.9 %all-gather = f32[64,6,16]{2,0,1:T(8,128)S(1)} all-gather(f32[32,6,16]{2,0,1:T(8,128)S(1)} %copy.249), channel_id=2, replica_groups=mesh['groups'=2,'blk'=4,'head'=2,'pair'=2] {'pair'}, dimensions={0}, use_global_device_ids=true | all-gather | bytes 36864 | tf_op jit(solution)/shard_map/all_gather | solution.py:18
  56.0 2.4 %all-gather.3 = f32[64,6,8,3]{2,1,3,0:T(8,128)S(1)} all-gather(f32[32,6,8,3]{2,1,3,0:T(8,128)S(1)} %copy.250), channel_id=5, replica_groups=mesh['groups'=2,'blk'=4,'head'=2,'pair'=2] {'pair'}, dimensions={0}, use_global_device_ids=true | all-gather | bytes 55296 | tf_op jit(solution)/shard_map/all_gather | solution.py:18
  58.6 1.1 %fusion.82 = (bf16[32,6,8,3]{2,3,1,0:T(4,128)(2,1)S(1)}, f32[32,6,8]{2,1,0:T(8,128)S(1)}) fusion(f32[3,3,32,1]{0,1,3,2:T(4,128)S(1)} %copy.271, f32[32,6,8,3]{2,1,3,0:T(8,128)S(1)} %fusion.30), kind=kOutput, calls=%fused_computation.152 | convolution fusion | flops 178176 | bytes 34944 | tf_op jit(solution)/shard_map/abn,nhpa->nhpb/dot_general | solution.py:34
  60.3 0.4 convolution_bitcast_fusion.4
  60.7 4.8 %all-gather.5 = f32[64,384]{1,0:T(8,128)S(1)} all-gather(f32[32,384]{1,0:T(8,128)S(1)} %convolution_bitcast_fusion.4), channel_id=7, replica_groups=mesh['groups'=2,'blk'=4,'head'=2,'pair'=2] {'head'}, dimensions={0}, use_global_device_ids=true | all-gather | bytes 147456 | tf_op jit(solution)/shard_map/all_gather | solution.py:223
  65.9 0.6 copy-done.11
  66.6 0.4 copy-done.5
  67.3 0.3 convolution_bitcast_fusion.3
  67.8 13.1 %all-gather.8 = f32[4,32,12]{1,2,0:T(8,128)S(1)} all-gather(f32[1,32,12]{1,2,0:T(8,128)S(1)} %maximum_bitcast_fusion), channel_id=1, replica_groups=mesh['groups'=2,'blk'=4,'head'=2,'pair'=2] {'blk'}, dimensions={0}, use_global_device_ids=true | all-gather | bytes 7680 | tf_op jit(solution)/shard_map/all_gather | solution.py:231
  80.9 0.7 reshape.715
  (177 shorter events, 11.9 us)
Async XLA Ops:
  0.6 59.6 %copy-start = (bf16[6,176,384]{2,1,0:T(8,128)(2,1)S(1)}, bf16[6,176,384]{2,1,0:T(8,128)(2,1)}, u32[]{:S(2)}) copy-start(bf16[6,176,384]{2,1,0:T(8,128)(2,1)} %param.29) | copy-start | bytes 2433028
  0.7 0.7 copy-start.13
  0.7 0.7 copy-start.14
  0.7 0.7 copy-start.15
  1.4 0.7 copy-start.8
  2.4 0.7 copy-start.3
  3.1 1.2 %copy-start.9 = (bf16[384,72]{0,1:T(8,128)(2,1)S(1)}, bf16[384,72]{0,1:T(8,128)(2,1)}, u32[]{:S(2)}) copy-start(bf16[384,72]{0,1:T(8,128)(2,1)} %param.24) | copy-start | bytes 165892
  4.5 0.9 %copy-start.7 = (bf16[384,96]{0,1:T(8,128)(2,1)S(1)}, bf16[384,96]{0,1:T(8,128)(2,1)}, u32[]{:S(2)}) copy-start(bf16[384,96]{0,1:T(8,128)(2,1)} %param.22) | copy-start | bytes 221188
  6.5 0.9 %copy-start.4 = (bf16[384,216]{0,1:T(8,128)(2,1)S(1)}, bf16[384,216]{0,1:T(8,128)(2,1)}, u32[]{:S(2)}) copy-start(bf16[384,216]{0,1:T(8,128)(2,1)} %param.25) | copy-start | bytes 497668
  7.6 1.0 %copy-start.2 = (bf16[32,4,16,128]{3,2,1,0:T(8,128)(2,1)S(1)}, bf16[32,4,16,128]{3,2,1,0:T(8,128)(2,1)}, u32[]{:S(2)}) copy-start(bf16[32,4,16,128]{3,2,1,0:T(8,128)(2,1)} %param.18) | copy-start | bytes 1572868
  8.3 0.7 copy-start.6
  9.8 0.7 copy-start.10
  12.0 6.7 %collective-permute-start = (f32[16,2]{0,1:T(2,128)S(1)}, f32[16,2]{0,1:T(2,128)S(1)}, u32[]{:S(2)}, u32[]{:S(2)}) collective-permute-start(f32[16,2]{0,1:T(2,128)S(1)} %get-tuple-element.757), channel_id=1, source_target_pairs={{0,4},{4,8},{8,12},{12,0},{1,5},{5,9},{9,13},{13,1},{2,6},{6,10},{... | collective-permute-start | bytes 392 | tf_op jit(solution)/shard_map/while/body/eval_jaxpr/ppermute | solution.py:14
  15.1 8.4 %collective-permute-start.1 = (f32[16,408]{0,1:T(8,128)S(1)}, f32[16,408]{0,1:T(8,128)S(1)}, u32[]{:S(2)}, u32[]{:S(2)}) collective-permute-start(f32[16,408]{0,1:T(8,128)S(1)} %get-tuple-element.756), channel_id=1, source_target_pairs={{0,4},{4,8},{8,12},{12,0},{1,5},{5,9},{9,13},{13,1},{2,6},{6,10},{... | collective-permute-start | bytes 78344 | tf_op jit(solution)/shard_map/while/body/eval_jaxpr/ppermute | solution.py:14
  23.6 0.7 copy-start.1
  25.0 0.9 %slice-start = ((f32[16,6,12,3]{0,3,2,1:T(4,128)}), f32[16,6,8,3]{0,3,2,1:T(4,128)S(1)}, s32[]{:S(2)}) async-start(f32[16,6,12,3]{0,3,2,1:T(4,128)} %copy-done.1), calls=%async_computation | async-start | bytes 196608 | tf_op jit(solution)/shard_map/while/body/eval_jaxpr/slice | solution.py:182
  26.4 5.4 %collective-permute-start = (f32[16,2]{0,1:T(2,128)S(1)}, f32[16,2]{0,1:T(2,128)S(1)}, u32[]{:S(2)}, u32[]{:S(2)}) collective-permute-start(f32[16,2]{0,1:T(2,128)S(1)} %get-tuple-element.757), channel_id=1, source_target_pairs={{0,4},{4,8},{8,12},{12,0},{1,5},{5,9},{9,13},{13,1},{2,6},{6,10},{... | collective-permute-start | bytes 392 | tf_op jit(solution)/shard_map/while/body/eval_jaxpr/ppermute | solution.py:14
  26.5 7.7 %collective-permute-start.1 = (f32[16,408]{0,1:T(8,128)S(1)}, f32[16,408]{0,1:T(8,128)S(1)}, u32[]{:S(2)}, u32[]{:S(2)}) collective-permute-start(f32[16,408]{0,1:T(8,128)S(1)} %get-tuple-element.756), channel_id=1, source_target_pairs={{0,4},{4,8},{8,12},{12,0},{1,5},{5,9},{9,13},{13,1},{2,6},{6,10},{... | collective-permute-start | bytes 78344 | tf_op jit(solution)/shard_map/while/body/eval_jaxpr/ppermute | solution.py:14
  34.2 0.7 copy-start.1
  35.6 0.9 %slice-start = ((f32[16,6,12,3]{0,3,2,1:T(4,128)}), f32[16,6,8,3]{0,3,2,1:T(4,128)S(1)}, s32[]{:S(2)}) async-start(f32[16,6,12,3]{0,3,2,1:T(4,128)} %copy-done.1), calls=%async_computation | async-start | bytes 196608 | tf_op jit(solution)/shard_map/while/body/eval_jaxpr/slice | solution.py:182
  37.0 5.4 %collective-permute-start = (f32[16,2]{0,1:T(2,128)S(1)}, f32[16,2]{0,1:T(2,128)S(1)}, u32[]{:S(2)}, u32[]{:S(2)}) collective-permute-start(f32[16,2]{0,1:T(2,128)S(1)} %get-tuple-element.757), channel_id=1, source_target_pairs={{0,4},{4,8},{8,12},{12,0},{1,5},{5,9},{9,13},{13,1},{2,6},{6,10},{... | collective-permute-start | bytes 392 | tf_op jit(solution)/shard_map/while/body/eval_jaxpr/ppermute | solution.py:14
  37.1 7.7 %collective-permute-start.1 = (f32[16,408]{0,1:T(8,128)S(1)}, f32[16,408]{0,1:T(8,128)S(1)}, u32[]{:S(2)}, u32[]{:S(2)}) collective-permute-start(f32[16,408]{0,1:T(8,128)S(1)} %get-tuple-element.756), channel_id=1, source_target_pairs={{0,4},{4,8},{8,12},{12,0},{1,5},{5,9},{9,13},{13,1},{2,6},{6,10},{... | collective-permute-start | bytes 78344 | tf_op jit(solution)/shard_map/while/body/eval_jaxpr/ppermute | solution.py:14
  44.8 0.7 copy-start.1
  46.1 0.9 %slice-start = ((f32[16,6,12,3]{0,3,2,1:T(4,128)}), f32[16,6,8,3]{0,3,2,1:T(4,128)S(1)}, s32[]{:S(2)}) async-start(f32[16,6,12,3]{0,3,2,1:T(4,128)} %copy-done.1), calls=%async_computation | async-start | bytes 196608 | tf_op jit(solution)/shard_map/while/body/eval_jaxpr/slice | solution.py:182
  60.7 5.1 %copy-start.12 = (f32[384]{0:T(512)S(1)}, f32[384]{0:T(512)}, u32[]{:S(2)}) copy-start(f32[384]{0:T(512)} %param.30) | copy-start | bytes 4612
  65.8 0.7 copy-start.11
  66.5 0.6 copy-start.5
